TPU v7x, 32 devices: a whole 2x2x4 slice. The times are simulated.
32 devices in a mesh: tm: 8 (over z, x), rows: 4 (over y, core).
Axes of the slice: x: 2, y: 2, z: 4, core: 2. Of those that a mesh axis runs over, the one named last changes fastest.
Arguments:
- clip: float32 [32, 8, 32, 128], P('tm', 'rows'), may hold values from -6 to 6
- kernel_one: float32 [3, 3, 3, 128, 128], replicated, may hold values from -0.109375 to 0.109375
- kernel_two: float32 [3, 3, 3, 128, 128], replicated, may hold values from -0.109375 to 0.109375
- cotangent: float32 [32, 8, 32, 128], P('tm', 'rows'), may hold values from -6 to 6
Outputs:
- block_out: float32 [32, 8, 32, 128], P('tm', 'rows')
- grad_clip: float32 [32, 8, 32, 128], P('tm', 'rows')
- grad_one: float32 [3, 3, 3, 128, 128], replicated
- grad_two: float32 [3, 3, 3, 128, 128], replicated
All inputs are finite; a program needn't handle non-finite values.
Results may differ from a plain program's by a relative error of at most 0.00014.
Values sent between devices are 32-bit elements; how exact they have to be, the bound alone decides.
No kernel may reach another device: no remote copies, remote signals or barrier semaphores. Data moves between devices by JAX's collectives and lax.ppermute only.
A program may use at most 128 MiB of HBM per device.

v0:
```python
import math
import jax
import jax.numpy as jnp
from jax import lax
from jax.sharding import PartitionSpec as P


def passed_along(value, axis, steps):
    count = lax.axis_size(axis)
    first, last = (max(0, -steps), min(count, count - steps))
    return lax.ppermute(value, axis, [(source, source + steps) for source in range(first, last)])


def padded_2(cells, sides, width):
    for axis, dim in sides:
        count = lax.axis_size(axis)
        ends = count - 1
        head = lax.slice_in_dim(cells, 0, width, axis=dim)
        tail = lax.slice_in_dim(cells, cells.shape[dim] - width, cells.shape[dim], axis=dim)
        cells = jnp.concatenate(
            [
                lax.ppermute(tail, axis, [(i, (i + 1) % count) for i in range(ends)]),
                cells,
                lax.ppermute(head, axis, [((i + 1) % count, i) for i in range(ends)]),
            ],
            axis=dim,
        )
    return cells


def columns(padded, step_time, step_row, out_frames, out_rows, span):
    window_piece = padded[step_time : step_time + out_frames, step_row : step_row + out_rows]
    joined = jnp.concatenate(
        [window_piece[:, :, offset : offset + span] for offset in range(3)], -1
    )
    return joined.reshape(out_frames * out_rows * span, -1)


def conv_local(extended, kernel):
    out_frames = extended.shape[0] - 2
    out_rows = extended.shape[1] - 2
    span = extended.shape[2]
    channels = extended.shape[3]
    padded = jnp.pad(extended, ((0, 0), (0, 0), (1, 1), (0, 0)))
    running = jnp.zeros((out_frames * out_rows * span, kernel.shape[-1]), jnp.float32)
    for step_time in range(3):
        for step_row in range(3):
            running = running + jnp.dot(
                columns(padded, step_time, step_row, out_frames, out_rows, span),
                kernel[step_time, step_row].reshape(3 * channels, -1),
                precision=lax.Precision.HIGHEST,
            )
    return running.reshape(out_frames, out_rows, span, -1)


def kernel_grad(extended, partner):
    out_frames = extended.shape[0] - 2
    out_rows = extended.shape[1] - 2
    span = extended.shape[2]
    channels = extended.shape[3]
    padded = jnp.pad(extended, ((0, 0), (0, 0), (1, 1), (0, 0)))
    flat_partner = partner.reshape(-1, partner.shape[-1])
    blocks = []
    for step_time in range(3):
        for step_row in range(3):
            product = lax.dot_general(
                columns(padded, step_time, step_row, out_frames, out_rows, span),
                flat_partner,
                (((0,), (0,)), ((), ())),
                precision=lax.Precision.HIGHEST,
            )
            blocks.append(product.reshape(3, channels, -1))
    return jnp.stack(blocks).reshape(3, 3, 3, channels, -1)


def flipped(kernel):
    return jnp.transpose(kernel[::-1, ::-1, ::-1], (0, 1, 2, 4, 3))


def frames_after(field):
    later = passed_along(field[:2], "tm", -1)
    return jnp.concatenate([field, later], 0)


def with_rims(field):
    return padded_2(field, (("rows", 1),), 1)


def per_device(clip, kernel_one, kernel_two, cotangent):
    frames, rows_here, span, channels = clip.shape
    height = rows_here * lax.axis_size("rows")
    factor = 1.0 / math.sqrt(frames * lax.axis_size("tm") * height * span)
    earlier = passed_along(clip, "tm", 1)
    deep_ext = padded_2(jnp.concatenate([earlier, clip], 0), (("rows", 1),), 2)
    pre_wide = conv_local(deep_ext, kernel_one)
    row_ids = lax.axis_index("rows") * rows_here - 1 + jnp.arange(rows_here + 2, dtype=jnp.int32)
    inside = ((row_ids >= 0) & (row_ids < height)).astype(jnp.float32)
    active_ext = jax.nn.silu(pre_wide) * inside[None, :, None, None]
    pre_one = pre_wide[2:, 1:-1]
    clip_ext = deep_ext[2:, 1:-1]
    block_out = clip + conv_local(active_ext, kernel_two)
    grad_ext = with_rims(frames_after(cotangent))
    d_active = conv_local(grad_ext, flipped(kernel_two))
    sigma = jax.nn.sigmoid(pre_one)
    delta = d_active * sigma * (1.0 + pre_one * (1.0 - sigma))
    grad_two = kernel_grad(active_ext, cotangent) * factor
    delta_ext = with_rims(frames_after(delta))
    grad_clip = cotangent + conv_local(delta_ext, flipped(kernel_one))
    grad_one = kernel_grad(clip_ext, delta) * factor
    grad_one, grad_two = lax.psum((grad_one, grad_two), ("tm", "rows"))
    return (block_out, grad_clip, grad_one, grad_two)


def solution(mesh):
    return jax.shard_map(
        per_device,
        mesh=mesh,
        in_specs=(P("tm", "rows", None, None), P(), P(), P("tm", "rows", None, None)),
        out_specs=(P("tm", "rows", None, None), P("tm", "rows", None, None), P(), P()),
        check_vma=False,
    )
```

profile of v0, /device:TPU:0, one launch (start us, length us, event | category | flops | bytes accessed | tf_op | source)
XLA Modules:
  0.0 273.9 jit_solution(3849822694402859812)
XLA Ops:
  7.2 5.5 %collective-permute-start = (f32[4,2,32,128]{3,2,1,0:T(8,128)}, f32[4,2,32,128]{3,2,1,0:T(8,128)}, u32[]{:S(2)}, u32[]{:S(2)}) collective-permute-start(f32[4,2,32,128]{3,2,1,0:T(8,128)} %param.4), channel_id=1, source_target_pairs={{0,4},{4,8},{8,12},{12,16},{16,20},{20,24},{24,28},{1,5},{5,9},{9,... | collective-permute-start | bytes 393224 | tf_op jit(solution)/shard_map/ppermute | solution.py:11
  12.7 1.5 slice.904
  14.2 1.3 collective-permute-start.3
  15.5 1.6 constant_dynamic-update-slice_fusion.3
  17.1 2.8 %fusion.48 = (f32[1,1,3,128,128]{4,3,2,1,0:T(8,128)}, f32[1,1,3,128,128]{4,3,2,1,0:T(8,128)}, f32[1,1,3,128,128]{4,3,2,1,0:T(8,128)}, f32[1,1,3,128,128]{4,3,2,1...) fusion(f32[3,3,3,128,128]{4,3,2,1,0:T(8,128)} %param.6), kind=kLoop, calls=%fused_computation.252 | loop fusion | bytes 3538944 | tf_op jit(solution)/shard_map/slice | solution.py:50
  19.9 2.0 copy.26
  21.9 1.2 fusion.49
  23.1 1.5 copy.27
  24.7 1.7 reverse_bitcast_fusion.1
  26.6 1.3 fusion.46
  28.8 1.3 collective-permute-start.5
  30.1 3.0 %collective-permute-start.4 = (f32[6,1,32,128]{3,2,1,0:T(8,128)S(1)}, f32[6,1,32,128]{3,2,1,0:T(8,128)S(1)}, u32[]{:S(2)}, u32[]{:S(2)}) collective-permute-start(f32[6,1,32,128]{3,2,1,0:T(8,128)S(1)} %get-tuple-element.185), channel_id=1, source_target_pairs={{0,1},{1,2},{2,3},{4,5},{5,6},{6,7},{8,9},{9,10},{10,11},{12,13},{... | collective-permute-start | bytes 294920 | tf_op jit(solution)/shard_map/ppermute | solution.py:22
  34.1 1.3 collective-permute-start.2
  35.4 4.1 %collective-permute-start.1 = (f32[8,2,32,128]{3,2,1,0:T(8,128)S(1)}, f32[8,2,32,128]{3,2,1,0:T(8,128)S(1)}, u32[]{:S(2)}, u32[]{:S(2)}) collective-permute-start(f32[8,2,32,128]{3,2,1,0:T(8,128)S(1)} %constant_dynamic-update-slice_fusion), channel_id=1, source_target_pairs={{0,1},{1,2},{2,3},{4,5},{5,6},{6,7},{8,9},{9,10},{10,11},{12,13},{... | collective-permute-start | bytes 786440 | tf_op jit(solution)/shard_map/ppermute | solution.py:22
  44.9 1.0 pad_slice_fusion.1
  47.2 1.2 fusion.58
  48.4 1.2 convolution_add_fusion.7
  50.5 1.2 convolution_add_fusion.6
  51.7 1.2 convolution_add_fusion.5
  53.8 14.2 %convolution_add_fusion.4 = f32[768,128]{1,0:T(8,128)S(1)} fusion(f32[768,128]{1,0:T(8,128)S(1)} %convolution_add_fusion.5, f32[768,384]{1,0:T(8,128)S(1)} %bitcast.357, f32[384,128]{1,0:T(8,128)S(1)} %bitcast.429), kind=kOutput, calls=%fused_computation.24 | convolution fusion | flops 453083136 | bytes 2162688 | tf_op jit(solution)/shard_map/dot_general | solution.py:48
  68.0 1.2 convolution_add_fusion.3
  70.1 1.2 convolution_add_fusion.2
  71.3 1.1 convolution_add_fusion.1
  73.4 1.1 convolution_add_fusion
  74.6 1.4 pad_slice_fusion.57
  76.1 1.0 fusion.53
  77.0 1.3 pad_slice_fusion.39
  78.4 0.9 copy.37
  79.3 1.1 fusion.59
  80.5 1.4 collective-permute-start.6
  83.9 1.0 pad_maximum_fusion.40
  85.9 1.1 pad_maximum_fusion.42
  87.3 1.3 pad_maximum_fusion.44
  89.8 1.2 copy.36
  95.4 1.4 broadcast_multiply_fusion.1
  98.9 1.0 copy.40
  100.9 0.9 copy.42
  102.8 0.9 copy.44
  103.8 1.1 pad_maximum_fusion.23
  104.8 0.9 copy.45
  105.8 1.5 fusion.8
  107.3 1.5 fusion.7
  112.4 1.6 broadcast_multiply_fusion
  118.7 1.3 collective-permute-start.8
  120.0 4.3 %collective-permute-start.7 = (f32[6,1,32,128]{3,2,1,0:T(8,128)S(1)}, f32[6,1,32,128]{3,2,1,0:T(8,128)S(1)}, u32[]{:S(2)}, u32[]{:S(2)}) collective-permute-start(f32[6,1,32,128]{3,2,1,0:T(8,128)S(1)} %get-tuple-element.175), channel_id=1, source_target_pairs={{0,1},{1,2},{2,3},{4,5},{5,6},{6,7},{8,9},{9,10},{10,11},{12,13},{... | collective-permute-start | bytes 294920 | tf_op jit(solution)/shard_map/ppermute | solution.py:22
  132.7 129.8 %all-reduce.8.cloned.1.call-done = (f32[3,3,3,128,128]{4,3,2,1,0:T(8,128)}, f32[3,3,3,128,128]{4,3,2,1,0:T(8,128)}) async-done(((f32[3,3,3,128,128]{4,3,2,1,0:T(8,128)}, f32[3,3,3,128,128]{4,3,2,1,0:T(8,128)}), (f32[3,3,3,128,128]{4,3,2,1,0:T(8,128)}, f32[3,3,3,128,128]{4,3,2,1,0:T(8,128)})) %all-reduce.8.cloned.1.call-update) | async-done | bytes 3538960 | tf_op jit(solution)/shard_map/psum | solution.py:110
  262.6 3.0 %copy.66 = f32[3,3,3,128,128]{4,3,2,1,0:T(8,128)} copy(f32[3,3,3,128,128]{4,3,2,1,0:T(8,128)} %get-tuple-element.213) | data formatting | bytes 3538944
  265.6 1.2 copy.67
  (265 shorter events, 41.4 us)
Async XLA Ops:
  7.2 255.4 %all-reduce.8.cloned.1.call-start = ((), (), s32[]{:S(2)}) async-start(), calls=%async_computation | async-start | bytes 7077888 | tf_op jit(solution)/shard_map/psum | solution.py:110
  7.2 25.9 %collective-permute-start = (f32[4,2,32,128]{3,2,1,0:T(8,128)}, f32[4,2,32,128]{3,2,1,0:T(8,128)}, u32[]{:S(2)}, u32[]{:S(2)}) collective-permute-start(f32[4,2,32,128]{3,2,1,0:T(8,128)} %param.4), channel_id=1, source_target_pairs={{0,4},{4,8},{8,12},{12,16},{16,20},{20,24},{24,28},{1,5},{5,9},{9,... | collective-permute-start | bytes 393224 | tf_op jit(solution)/shard_map/ppermute | solution.py:11
  14.2 13.7 %collective-permute-start.3 = (f32[2,2,32,128]{3,2,1,0:T(8,128)}, f32[2,2,32,128]{3,2,1,0:T(8,128)}, u32[]{:S(2)}, u32[]{:S(2)}) collective-permute-start(f32[2,2,32,128]{3,2,1,0:T(8,128)} %slice.904), channel_id=1, source_target_pairs={{4,0},{8,4},{12,8},{16,12},{20,16},{24,20},{28,24},{5,1},{9,5},{13... | collective-permute-start | bytes 196616 | tf_op jit(solution)/shard_map/ppermute | solution.py:11
  17.1 2.9 %copy-start.1 = (f32[3,3,3,128,128]{4,3,2,1,0:T(8,128)S(1)}, f32[3,3,3,128,128]{4,3,2,1,0:T(8,128)}, u32[]{:S(2)}) copy-start(f32[3,3,3,128,128]{4,3,2,1,0:T(8,128)} %param.6) | copy-start | bytes 5308420
  19.9 2.0 copy-start.2
  26.6 7.4 %copy-start.13 = (f32[4,2,32,128]{3,2,1,0:T(8,128)S(1)}, f32[4,2,32,128]{3,2,1,0:T(8,128)}, u32[]{:S(2)}) copy-start(f32[4,2,32,128]{3,2,1,0:T(8,128)} %param.4) | copy-start | bytes 393220
  28.8 10.7 %collective-permute-start.5 = (f32[6,1,32,128]{3,2,1,0:T(8,128)S(1)}, f32[6,1,32,128]{3,2,1,0:T(8,128)S(1)}, u32[]{:S(2)}, u32[]{:S(2)}) collective-permute-start(f32[6,1,32,128]{3,2,1,0:T(8,128)S(1)} %get-tuple-element.186), channel_id=1, source_target_pairs={{1,0},{2,1},{3,2},{5,4},{6,5},{7,6},{9,8},{10,9},{11,10},{13,12},{... | collective-permute-start | bytes 294920 | tf_op jit(solution)/shard_map/ppermute | solution.py:24
  30.1 9.4 %collective-permute-start.4 = (f32[6,1,32,128]{3,2,1,0:T(8,128)S(1)}, f32[6,1,32,128]{3,2,1,0:T(8,128)S(1)}, u32[]{:S(2)}, u32[]{:S(2)}) collective-permute-start(f32[6,1,32,128]{3,2,1,0:T(8,128)S(1)} %get-tuple-element.185), channel_id=1, source_target_pairs={{0,1},{1,2},{2,3},{4,5},{5,6},{6,7},{8,9},{9,10},{10,11},{12,13},{... | collective-permute-start | bytes 294920 | tf_op jit(solution)/shard_map/ppermute | solution.py:22
  34.1 10.7 %collective-permute-start.2 = (f32[8,2,32,128]{3,2,1,0:T(8,128)S(1)}, f32[8,2,32,128]{3,2,1,0:T(8,128)S(1)}, u32[]{:S(2)}, u32[]{:S(2)}) collective-permute-start(f32[8,2,32,128]{3,2,1,0:T(8,128)S(1)} %constant_dynamic-update-slice_fusion), channel_id=1, source_target_pairs={{1,0},{2,1},{3,2},{5,4},{6,5},{7,6},{9,8},{10,9},{11,10},{13,12},{... | collective-permute-start | bytes 786440 | tf_op jit(solution)/shard_map/ppermute | solution.py:24
  35.4 9.4 %collective-permute-start.1 = (f32[8,2,32,128]{3,2,1,0:T(8,128)S(1)}, f32[8,2,32,128]{3,2,1,0:T(8,128)S(1)}, u32[]{:S(2)}, u32[]{:S(2)}) collective-permute-start(f32[8,2,32,128]{3,2,1,0:T(8,128)S(1)} %constant_dynamic-update-slice_fusion), channel_id=1, source_target_pairs={{0,1},{1,2},{2,3},{4,5},{5,6},{6,7},{8,9},{9,10},{10,11},{12,13},{... | collective-permute-start | bytes 786440 | tf_op jit(solution)/shard_map/ppermute | solution.py:22
  46.5 1.9 copy-start.22
  49.8 1.9 copy-start.20
  53.2 14.9 %copy-start.18 = (f32[1,1,3,128,128]{4,3,2,1,0:T(8,128)S(1)}, f32[1,1,3,128,128]{4,3,2,1,0:T(8,128)}, u32[]{:S(2)}) copy-start(f32[1,1,3,128,128]{4,3,2,1,0:T(8,128)} %get-tuple-element.36) | copy-start | bytes 589828
  69.5 1.9 copy-start.16
  80.4 2.4 copy-start.68
  80.4 2.4 copy-start.69
  80.4 2.4 copy-start.70
  80.4 2.4 copy-start.71
  80.4 2.4 copy-start.72
  80.4 2.4 copy-start.73
  80.5 38.1 %collective-permute-start.6 = (f32[2,2,32,128]{3,2,1,0:T(8,128)S(1)}, f32[2,2,32,128]{3,2,1,0:T(8,128)S(1)}, u32[]{:S(2)}, u32[]{:S(2)}) collective-permute-start(f32[2,2,32,128]{3,2,1,0:T(8,128)S(1)} %slice.1071), channel_id=1, source_target_pairs={{4,0},{8,4},{12,8},{16,12},{20,16},{24,20},{28,24},{5,1},{9,5},{13... | collective-permute-start | bytes 196616 | tf_op jit(solution)/shard_map/ppermute | solution.py:11
  96.9 1.9 copy-start.53
  96.9 1.9 copy-start.54
  96.9 1.9 copy-start.62
  97.9 2.0 copy-start.51
  97.9 2.0 copy-start.52
  97.9 2.0 copy-start.61
  98.9 2.0 copy-start.49
  98.9 2.0 copy-start.50
  98.9 2.0 copy-start.60
  99.9 2.0 copy-start.47
  99.9 2.0 copy-start.48
  99.9 2.0 copy-start.57
  100.9 1.9 copy-start.44
  100.9 1.9 copy-start.45
  100.9 1.9 copy-start.46
  105.8 3.1 %copy-start.5 = (f32[256,384]{0,1:T(8,128)S(1)}, f32[256,384]{0,1:T(8,128)}, u32[]{:S(2)}) copy-start(f32[256,384]{0,1:T(8,128)} %copy.39) | copy-start | bytes 1179652
  105.8 3.6 %copy-start.6 = (f32[256,384]{0,1:T(8,128)S(1)}, f32[256,384]{0,1:T(8,128)}, u32[]{:S(2)}) copy-start(f32[256,384]{0,1:T(8,128)} %copy.40) | copy-start | bytes 1179652
  107.3 2.6 copy-start.7
  108.9 1.5 copy-start.8
  109.4 1.5 copy-start.9
  112.3 1.6 copy-start.41
  112.4 1.6 copy-start.65
  112.4 2.1 copy-start.40
  118.7 5.6 %collective-permute-start.8 = (f32[6,1,32,128]{3,2,1,0:T(8,128)S(1)}, f32[6,1,32,128]{3,2,1,0:T(8,128)S(1)}, u32[]{:S(2)}, u32[]{:S(2)}) collective-permute-start(f32[6,1,32,128]{3,2,1,0:T(8,128)S(1)} %get-tuple-element.176), channel_id=1, source_target_pairs={{1,0},{2,1},{3,2},{5,4},{6,5},{7,6},{9,8},{10,9},{11,10},{13,12},{... | collective-permute-start | bytes 294920 | tf_op jit(solution)/shard_map/ppermute | solution.py:24
  120.0 5.2 %collective-permute-start.7 = (f32[6,1,32,128]{3,2,1,0:T(8,128)S(1)}, f32[6,1,32,128]{3,2,1,0:T(8,128)S(1)}, u32[]{:S(2)}, u32[]{:S(2)}) collective-permute-start(f32[6,1,32,128]{3,2,1,0:T(8,128)S(1)} %get-tuple-element.175), channel_id=1, source_target_pairs={{0,1},{1,2},{2,3},{4,5},{5,6},{6,7},{8,9},{9,10},{10,11},{12,13},{... | collective-permute-start | bytes 294920 | tf_op jit(solution)/shard_map/ppermute | solution.py:22
  127.7 1.9 copy-start.30
  262.6 3.0 %copy-start.4 = (f32[3,3,3,128,128]{4,3,2,1,0:T(8,128)S(1)}, f32[3,3,3,128,128]{4,3,2,1,0:T(8,128)}, u32[]{:S(2)}) copy-start(f32[3,3,3,128,128]{4,3,2,1,0:T(8,128)} %get-tuple-element.214) | copy-start | bytes 5308420
  (36 other events, 44.2 us)
Sparse Core Ops, SparseCore 0:
  118.8 143.7 all-reduce.7
where the time goes:
time: 277 us; the launch traced here: 274 us
  waiting for transfers between devices  131 us (47%)
  matrix products  47.7 us (17%)
  local copies, waits for them, and re-layouts  43.1 us (16%)
  starting transfers between devices  23.5 us (8%)
  between operations  15.8 us (6%)
  other arithmetic  13 us (5%)
    psum x1, waiting for transfers between devices, per_device(): grad_one, grad_two = lax.psum((grad_one, grad_two), ('tm', 'rows'))  130 us
    dot_general x36, matrix products, conv_local(): jnp.dot(columns(padded, step_time, step_row, out_frames, out_rows, span),...  37 us
    unnamed x154, local copies, waits for them, and re-layouts  16.7 us
    reshape x18, local copies, waits for them, and re-layouts, columns(): return joined.reshape(out_frames * out_rows * span, -1)  11.5 us
    ppermute x3, starting transfers between devices, padded_2(): lax.ppermute(tail, axis, [(i, (i + 1) % count) for i in range(ends)])  11.3 us
    dot_general x18, matrix products, kernel_grad(): lax.dot_general(columns(padded, step_time, step_row, out_frames, out_rows...  10.7 us
    ppermute x3, starting transfers between devices, passed_along(): lax.ppermute(value, axis, [(source, source + steps) for source in range(f...  8.24 us
    concatenate x30, other arithmetic, columns(): jnp.concatenate([window_piece[:, :, offset:offset + span] for offset in r...  6.96 us
  transfers between devices with their start and end apart: 10, of which 2 were waited for; matrix products, arithmetic and copies ran while one was open for 22% of the time, Pallas kernels for 0%

commit v1 on v0

--- a/solution.py
+++ b/solution.py
@@ -107,7 +107,7 @@
     delta_ext = with_rims(frames_after(delta))
     grad_clip = cotangent + conv_local(delta_ext, flipped(kernel_one))
     grad_one = kernel_grad(clip_ext, delta) * factor
-    grad_one, grad_two = lax.psum((grad_one, grad_two), ("tm", "rows"))
+    grad_one, grad_two = lax.psum(lax.psum((grad_one, grad_two), "rows"), "tm")
     return (block_out, grad_clip, grad_one, grad_two)
 
 

time: 277 us -> 354 us (1.28)
  waiting for transfers between devices: 131 us -> 204 us
    psum x1 -> x2, waiting for transfers between devices: 130 us -> 204 us  [per_device(): grad_one, grad_two = lax.psum(lax.psum((grad_one, grad_two), 'rows'), 'tm')]
    unnamed x154 -> x162, local copies, waits for them, and re-layouts: 16.7 us -> 15.9 us
  transfers between devices with their start and end apart: 10 -> 11, of which waited for: 2 -> 3; matrix products, arithmetic and copies ran while one was open for 22% -> 19% of each run, Pallas kernels for 0% -> 0%
where the time goes in v1:
time: 354 us; the launch traced here: 351 us
  waiting for transfers between devices  204 us (58%)
  matrix products  49.4 us (14%)
  local copies, waits for them, and re-layouts  43.1 us (12%)
  starting transfers between devices  23.4 us (7%)
  between operations  15.8 us (4%)
  other arithmetic  15.4 us (4%)
    psum x2, waiting for transfers between devices, per_device(): grad_one, grad_two = lax.psum(lax.psum((grad_one, grad_two), 'rows'), 'tm')  204 us
    dot_general x36, matrix products, conv_local(): jnp.dot(columns(padded, step_time, step_row, out_frames, out_rows, span),...  37.6 us
    unnamed x162, local copies, waits for them, and re-layouts  15.9 us
    dot_general x18, matrix products, kernel_grad(): lax.dot_general(columns(padded, step_time, step_row, out_frames, out_rows...  11.8 us
    reshape x18, local copies, waits for them, and re-layouts, columns(): return joined.reshape(out_frames * out_rows * span, -1)  11.6 us
    ppermute x3, starting transfers between devices, padded_2(): lax.ppermute(tail, axis, [(i, (i + 1) % count) for i in range(ends)])  11.4 us
    concatenate x30, other arithmetic, columns(): jnp.concatenate([window_piece[:, :, offset:offset + span] for offset in r...  8.87 us
    ppermute x3, starting transfers between devices, passed_along(): lax.ppermute(value, axis, [(source, source + steps) for source in range(f...  8.1 us
  transfers between devices with their start and end apart: 11, of which 3 were waited for; matrix products, arithmetic and copies ran while one was open for 19% of the time, Pallas kernels for 0%

profile of v1, /device:TPU:0, one launch (start us, length us, event | category | flops | bytes accessed | tf_op | source)
XLA Modules:
  0.0 351.1 jit_solution(16741174536551765278)
XLA Ops:
  7.2 5.5 %collective-permute-start = (f32[4,2,32,128]{3,2,1,0:T(8,128)}, f32[4,2,32,128]{3,2,1,0:T(8,128)}, u32[]{:S(2)}, u32[]{:S(2)}) collective-permute-start(f32[4,2,32,128]{3,2,1,0:T(8,128)} %param.4), channel_id=1, source_target_pairs={{0,4},{4,8},{8,12},{12,16},{16,20},{20,24},{24,28},{1,5},{5,9},{9,... | collective-permute-start | bytes 393224 | tf_op jit(solution)/shard_map/ppermute | solution.py:11
  12.7 1.5 slice.904
  14.2 1.3 collective-permute-start.3
  15.5 1.6 constant_dynamic-update-slice_fusion.3
  17.1 2.9 fusion.48
  20.0 2.0 copy.26
  22.0 1.2 fusion.49
  23.2 1.5 copy.27
  24.7 1.7 reverse_bitcast_fusion.1
  26.7 1.3 fusion.46
  28.8 1.3 collective-permute-start.5
  30.1 3.0 collective-permute-start.4
  34.1 1.3 collective-permute-start.2
  35.4 4.1 %collective-permute-start.1 = (f32[8,2,32,128]{3,2,1,0:T(8,128)S(1)}, f32[8,2,32,128]{3,2,1,0:T(8,128)S(1)}, u32[]{:S(2)}, u32[]{:S(2)}) collective-permute-start(f32[8,2,32,128]{3,2,1,0:T(8,128)S(1)} %constant_dynamic-update-slice_fusion), channel_id=1, source_target_pairs={{0,1},{1,2},{2,3},{4,5},{5,6},{6,7},{8,9},{9,10},{10,11},{12,13},{... | collective-permute-start | bytes 786440 | tf_op jit(solution)/shard_map/ppermute | solution.py:22
  44.9 1.0 pad_slice_fusion.1
  47.3 1.2 fusion.58
  48.5 1.2 convolution_add_fusion.7
  50.6 1.2 convolution_add_fusion.6
  51.8 1.2 convolution_add_fusion.5
  53.9 14.2 %convolution_add_fusion.4 = f32[768,128]{1,0:T(8,128)S(1)} fusion(f32[768,128]{1,0:T(8,128)S(1)} %convolution_add_fusion.5, f32[768,384]{1,0:T(8,128)S(1)} %bitcast.357, f32[384,128]{1,0:T(8,128)S(1)} %bitcast.429), kind=kOutput, calls=%fused_computation.24 | convolution fusion | flops 453083136 | bytes 2162688 | tf_op jit(solution)/shard_map/dot_general | solution.py:48
  68.1 1.2 convolution_add_fusion.3
  70.2 1.2 convolution_add_fusion.2
  71.4 1.1 convolution_add_fusion.1
  72.7 1.1 convolution_add_fusion
  73.9 1.4 pad_slice_fusion.57
  76.3 1.3 pad_slice_fusion.39
  77.6 1.0 copy.37
  78.6 1.1 fusion.59
  79.8 1.3 collective-permute-start.6
  83.0 1.0 pad_maximum_fusion.40
  84.4 1.1 pad_maximum_fusion.42
  85.9 1.3 pad_maximum_fusion.44
  88.4 1.2 copy.36
  94.0 1.4 broadcast_multiply_fusion.1
  99.4 1.0 pad_maximum_fusion.20
  104.1 1.1 pad_maximum_fusion.23
  106.1 1.6 fusion.8
  107.7 1.5 fusion.7
  109.2 1.5 fusion.6
  113.8 1.4 broadcast_multiply_fusion
  116.2 1.1 convolution_add_fusion.29
  121.5 1.3 collective-permute-start.8
  122.8 4.3 %collective-permute-start.7 = (f32[6,1,32,128]{3,2,1,0:T(8,128)S(1)}, f32[6,1,32,128]{3,2,1,0:T(8,128)S(1)}, u32[]{:S(2)}, u32[]{:S(2)}) collective-permute-start(f32[6,1,32,128]{3,2,1,0:T(8,128)S(1)} %get-tuple-element.177), channel_id=1, source_target_pairs={{0,1},{1,2},{2,3},{4,5},{5,6},{6,7},{8,9},{9,10},{10,11},{12,13},{... | collective-permute-start | bytes 294920 | tf_op jit(solution)/shard_map/ppermute | solution.py:22
  128.1 1.0 fusion.51
  129.1 68.3 %all-reduce.12.cloned.1.call-done = (f32[3,3,3,128,128]{4,3,2,1,0:T(8,128)}, f32[3,3,3,128,128]{4,3,2,1,0:T(8,128)}) async-done(((f32[3,3,3,128,128]{4,3,2,1,0:T(8,128)}, f32[3,3,3,128,128]{4,3,2,1,0:T(8,128)}), (f32[3,3,3,128,128]{4,3,2,1,0:T(8,128)}, f32[3,3,3,128,128]{4,3,2,1,0:T(8,128)})) %all-reduce.12.cloned.1.call-update) | async-done | bytes 3538960 | tf_op jit(solution)/shard_map/psum | solution.py:110
  204.5 135.4 %all-reduce.10.cloned.1.call-done = (f32[3,3,3,128,128]{4,3,2,1,0:T(8,128)}, f32[3,3,3,128,128]{4,3,2,1,0:T(8,128)}) async-done(((f32[3,3,3,128,128]{4,3,2,1,0:T(8,128)}, f32[3,3,3,128,128]{4,3,2,1,0:T(8,128)}), (f32[3,3,3,128,128]{4,3,2,1,0:T(8,128)}, f32[3,3,3,128,128]{4,3,2,1,0:T(8,128)})) %all-reduce.10.cloned.1.call-update) | async-done | bytes 3538960 | tf_op jit(solution)/shard_map/psum | solution.py:110
  339.8 3.0 copy.68
  342.8 1.2 copy.69
  (276 shorter events, 45.0 us)
Async XLA Ops:
  7.2 190.2 %all-reduce.12.cloned.1.call-start = ((), (), s32[]{:S(2)}) async-start(), calls=%async_computation.1 | async-start | bytes 7077888 | tf_op jit(solution)/shard_map/psum | solution.py:110
  7.2 26.0 %collective-permute-start = (f32[4,2,32,128]{3,2,1,0:T(8,128)}, f32[4,2,32,128]{3,2,1,0:T(8,128)}, u32[]{:S(2)}, u32[]{:S(2)}) collective-permute-start(f32[4,2,32,128]{3,2,1,0:T(8,128)} %param.4), channel_id=1, source_target_pairs={{0,4},{4,8},{8,12},{12,16},{16,20},{20,24},{24,28},{1,5},{5,9},{9,... | collective-permute-start | bytes 393224 | tf_op jit(solution)/shard_map/ppermute | solution.py:11
  14.2 13.7 %collective-permute-start.3 = (f32[2,2,32,128]{3,2,1,0:T(8,128)}, f32[2,2,32,128]{3,2,1,0:T(8,128)}, u32[]{:S(2)}, u32[]{:S(2)}) collective-permute-start(f32[2,2,32,128]{3,2,1,0:T(8,128)} %slice.904), channel_id=1, source_target_pairs={{4,0},{8,4},{12,8},{16,12},{20,16},{24,20},{28,24},{5,1},{9,5},{13... | collective-permute-start | bytes 196616 | tf_op jit(solution)/shard_map/ppermute | solution.py:11
  17.1 2.9 copy-start.1
  20.0 2.0 copy-start.2
  26.7 7.5 %copy-start.12 = (f32[4,2,32,128]{3,2,1,0:T(8,128)S(1)}, f32[4,2,32,128]{3,2,1,0:T(8,128)}, u32[]{:S(2)}) copy-start(f32[4,2,32,128]{3,2,1,0:T(8,128)} %param.4) | copy-start | bytes 393220
  28.8 10.7 %collective-permute-start.5 = (f32[6,1,32,128]{3,2,1,0:T(8,128)S(1)}, f32[6,1,32,128]{3,2,1,0:T(8,128)S(1)}, u32[]{:S(2)}, u32[]{:S(2)}) collective-permute-start(f32[6,1,32,128]{3,2,1,0:T(8,128)S(1)} %get-tuple-element.188), channel_id=1, source_target_pairs={{1,0},{2,1},{3,2},{5,4},{6,5},{7,6},{9,8},{10,9},{11,10},{13,12},{... | collective-permute-start | bytes 294920 | tf_op jit(solution)/shard_map/ppermute | solution.py:24
  30.1 9.4 %collective-permute-start.4 = (f32[6,1,32,128]{3,2,1,0:T(8,128)S(1)}, f32[6,1,32,128]{3,2,1,0:T(8,128)S(1)}, u32[]{:S(2)}, u32[]{:S(2)}) collective-permute-start(f32[6,1,32,128]{3,2,1,0:T(8,128)S(1)} %get-tuple-element.187), channel_id=1, source_target_pairs={{0,1},{1,2},{2,3},{4,5},{5,6},{6,7},{8,9},{9,10},{10,11},{12,13},{... | collective-permute-start | bytes 294920 | tf_op jit(solution)/shard_map/ppermute | solution.py:22
  34.1 10.7 %collective-permute-start.2 = (f32[8,2,32,128]{3,2,1,0:T(8,128)S(1)}, f32[8,2,32,128]{3,2,1,0:T(8,128)S(1)}, u32[]{:S(2)}, u32[]{:S(2)}) collective-permute-start(f32[8,2,32,128]{3,2,1,0:T(8,128)S(1)} %constant_dynamic-update-slice_fusion), channel_id=1, source_target_pairs={{1,0},{2,1},{3,2},{5,4},{6,5},{7,6},{9,8},{10,9},{11,10},{13,12},{... | collective-permute-start | bytes 786440 | tf_op jit(solution)/shard_map/ppermute | solution.py:24
  35.4 9.4 %collective-permute-start.1 = (f32[8,2,32,128]{3,2,1,0:T(8,128)S(1)}, f32[8,2,32,128]{3,2,1,0:T(8,128)S(1)}, u32[]{:S(2)}, u32[]{:S(2)}) collective-permute-start(f32[8,2,32,128]{3,2,1,0:T(8,128)S(1)} %constant_dynamic-update-slice_fusion), channel_id=1, source_target_pairs={{0,1},{1,2},{2,3},{4,5},{5,6},{6,7},{8,9},{9,10},{10,11},{12,13},{... | collective-permute-start | bytes 786440 | tf_op jit(solution)/shard_map/ppermute | solution.py:22
  53.2 14.9 %copy-start.17 = (f32[1,1,3,128,128]{4,3,2,1,0:T(8,128)S(1)}, f32[1,1,3,128,128]{4,3,2,1,0:T(8,128)}, u32[]{:S(2)}) copy-start(f32[1,1,3,128,128]{4,3,2,1,0:T(8,128)} %get-tuple-element.38) | copy-start | bytes 589828
  76.3 2.3 copy-start.24
  78.6 3.4 copy-start.72
  78.6 3.4 copy-start.73
  78.6 3.4 copy-start.74
  78.6 3.4 copy-start.75
  78.6 3.4 copy-start.76
  78.6 3.4 copy-start.77
  79.8 41.6 %collective-permute-start.6 = (f32[2,2,32,128]{3,2,1,0:T(8,128)S(1)}, f32[2,2,32,128]{3,2,1,0:T(8,128)S(1)}, u32[]{:S(2)}, u32[]{:S(2)}) collective-permute-start(f32[2,2,32,128]{3,2,1,0:T(8,128)S(1)} %slice.1071), channel_id=1, source_target_pairs={{4,0},{8,4},{12,8},{16,12},{20,16},{24,20},{28,24},{5,1},{9,5},{13... | collective-permute-start | bytes 196616 | tf_op jit(solution)/shard_map/ppermute | solution.py:11
  89.5 2.4 copy-start.10
  94.0 2.4 copy-start.58
  94.0 2.4 copy-start.59
  94.0 2.4 copy-start.64
  96.4 2.0 copy-start.54
  96.4 2.0 copy-start.55
  96.4 2.0 copy-start.62
  97.4 2.0 copy-start.53
  98.4 2.9 copy-start.50
  98.4 2.9 copy-start.51
  99.4 3.8 %copy-start.47 = (f32[4,2,32,128]{3,2,1,0:T(8,128)S(1)}, f32[4,2,32,128]{3,2,1,0:T(8,128)}, u32[]{:S(2)}) copy-start(f32[4,2,32,128]{3,2,1,0:T(8,128)} %get-tuple-element.143) | copy-start | bytes 393220
  99.4 3.8 %copy-start.48 = (f32[4,2,32,128]{3,2,1,0:T(8,128)S(1)}, f32[4,2,32,128]{3,2,1,0:T(8,128)}, u32[]{:S(2)}) copy-start(f32[4,2,32,128]{3,2,1,0:T(8,128)} %get-tuple-element.144) | copy-start | bytes 393220
  99.4 3.8 %copy-start.49 = (f32[4,2,32,128]{3,2,1,0:T(8,128)S(1)}, f32[4,2,32,128]{3,2,1,0:T(8,128)}, u32[]{:S(2)}) copy-start(f32[4,2,32,128]{3,2,1,0:T(8,128)} %get-tuple-element.147) | copy-start | bytes 393220
  106.1 4.7 %copy-start.5 = (f32[256,384]{0,1:T(8,128)S(1)}, f32[256,384]{0,1:T(8,128)}, u32[]{:S(2)}) copy-start(f32[256,384]{0,1:T(8,128)} %copy.40) | copy-start | bytes 1179652
  106.1 5.2 %copy-start.6 = (f32[256,384]{0,1:T(8,128)S(1)}, f32[256,384]{0,1:T(8,128)}, u32[]{:S(2)}) copy-start(f32[256,384]{0,1:T(8,128)} %copy.41) | copy-start | bytes 1179652
  106.1 5.7 %copy-start.7 = (f32[256,384]{0,1:T(8,128)S(1)}, f32[256,384]{0,1:T(8,128)}, u32[]{:S(2)}) copy-start(f32[256,384]{0,1:T(8,128)} %copy.42) | copy-start | bytes 1179652
  107.7 4.6 %copy-start.8 = (f32[256,384]{0,1:T(8,128)S(1)}, f32[256,384]{0,1:T(8,128)}, u32[]{:S(2)}) copy-start(f32[256,384]{0,1:T(8,128)} %copy.43) | copy-start | bytes 1179652
  109.2 3.5 %copy-start.9 = (f32[256,384]{0,1:T(8,128)S(1)}, f32[256,384]{0,1:T(8,128)}, u32[]{:S(2)}) copy-start(f32[256,384]{0,1:T(8,128)} %copy.44) | copy-start | bytes 1179652
  110.8 2.5 copy-start.11
  113.8 2.4 copy-start.38
  117.4 2.4 copy-start.34
  117.4 2.9 copy-start.33
  117.4 222.5 %all-reduce.10.cloned.1.call-start = ((), (), s32[]{:S(2)}) async-start(), calls=%async_computation | async-start | bytes 7077888 | tf_op jit(solution)/shard_map/psum | solution.py:110
  121.5 6.2 %collective-permute-start.8 = (f32[6,1,32,128]{3,2,1,0:T(8,128)S(1)}, f32[6,1,32,128]{3,2,1,0:T(8,128)S(1)}, u32[]{:S(2)}, u32[]{:S(2)}) collective-permute-start(f32[6,1,32,128]{3,2,1,0:T(8,128)S(1)} %get-tuple-element.178), channel_id=1, source_target_pairs={{1,0},{2,1},{3,2},{5,4},{6,5},{7,6},{9,8},{10,9},{11,10},{13,12},{... | collective-permute-start | bytes 294920 | tf_op jit(solution)/shard_map/ppermute | solution.py:24
  122.8 5.2 %collective-permute-start.7 = (f32[6,1,32,128]{3,2,1,0:T(8,128)S(1)}, f32[6,1,32,128]{3,2,1,0:T(8,128)S(1)}, u32[]{:S(2)}, u32[]{:S(2)}) collective-permute-start(f32[6,1,32,128]{3,2,1,0:T(8,128)S(1)} %get-tuple-element.177), channel_id=1, source_target_pairs={{0,1},{1,2},{2,3},{4,5},{5,6},{6,7},{8,9},{9,10},{10,11},{12,13},{... | collective-permute-start | bytes 294920 | tf_op jit(solution)/shard_map/ppermute | solution.py:22
  198.7 2.1 copy-start.30
  198.8 2.6 copy-start.29
  199.8 2.0 copy-start.28
  339.8 3.0 copy-start.4
  (41 other events, 58.7 us)
Sparse Core Ops, SparseCore 0:
  117.5 79.8 all-reduce.11
  201.0 138.8 all-reduce.9
